TPU v7x, 128 devices: a whole 4x4x4 slice. The times are simulated.
128 devices in a mesh: tu: 16 (over x, z), tv: 8 (over y, core).
Axes of the slice: x: 4, y: 4, z: 4, core: 2. Of those that a mesh axis runs over, the one named last changes fastest.
Arguments:
- aperture_amp: bfloat16 [512, 512, 512], P(('tu', 'tv')), may hold values from 0.19921875 to 1.796875
- aperture_phase: bfloat16 [512, 512, 512], P(('tu', 'tv')), may hold values from -3.140625 to 3.140625
- plane_depths: float32 [4], replicated, may hold values from 8 to 344
- send_list: int32 [128, 128, 2], P(('tu', 'tv')), may hold values from 0 to 15, as said below
- send_count: int32 [128, 128], P(('tu', 'tv')), may hold values from 0 to 2, as said below
- vis_left: bfloat16 [49152, 128, 128], P(('tu', 'tv')), may hold values from -0.078125 to 0.078125
- vis_right: bfloat16 [49152, 64, 128], P(('tu', 'tv')), may hold values from -0.75 to 0.75
- block_slot: int32 [49152], P(('tu', 'tv')), may hold values from 0 to 255, as said below
- block_pos: int32 [49152], P(('tu', 'tv')), may hold values from 0 to 31
- block_count: int32 [128], P(('tu', 'tv')), may hold values from 96 to 384, as said below
Outputs:
- uv_grid: float32 [2, 4096, 4096], P(None, 'tu', 'tv')
Inputs may be any that keep to these rules, and one draw needn't show every extreme that they name: `send_list`: each owner sends every one of its kernels to 8 slots, 128 in all; the used slots of an owner and tile are the first send_count of them; entries of unused slots are arbitrary kernel numbers in range. One tile, drawn afresh, receives 2 slots from every owner; a row of send_count sums to 128. `block_slot`: names a slot r = d * 2 + c that the block's tile receives, with c < send_count[d, tile]. `block_count`: some tile uses all 384 slots.
All inputs are finite; a program needn't handle non-finite values.
Results may differ from a plain program's by a relative error of at most 0.0065.
Values may be sent and summed in bfloat16 or wider, within the bound.
A program may use at most 192 MiB of HBM per device.

v0:
```python
import math
import random

import jax
import jax.numpy as jnp
import numpy as np
from jax import lax
from jax.experimental import pallas as pl
from jax.experimental.pallas import tpu as pltpu
from jax.sharding import PartitionSpec as P

SCREEN = 512
KSIZE = 64
PATCH = 128
PLANES = 4
SCREENS_DEV = 4
BLOCKS_DEV = 384
OWNERS = 128
TILE_U = 256
TILE_V = 512
POSITIONS = 32
GROUP = 4
MAX_GROUPS = BLOCKS_DEV // GROUP + POSITIONS
DEPTH = 6
EXT_U = TILE_U + KSIZE

SIN = (0.9999995827674866, -0.16666553914546967, 0.008332408033311367,
       -0.00019808740762528032, 2.6998227440344635e-06, -2.036623314438657e-08)
COS = (0.9999992251396179, -0.49999427795410156, 0.041659820824861526,
       -0.0013858915772289038, 2.4204400688176975e-05, -2.19788830690959e-07)


def sincos(x):
    z = x * x
    s = jnp.float32(SIN[-1])
    for c in SIN[-2::-1]:
        s = s * z + c
    k = jnp.float32(COS[-1])
    for c in COS[-2::-1]:
        k = k * z + c
    return s * x, k


def dft_rows():
    freq = np.arange(KSIZE) - KSIZE // 2
    turns = np.mod(freq[:, None] * np.arange(SCREEN)[None, :], SCREEN)
    angles = 2.0 * math.pi / SCREEN * turns
    return np.stack([np.cos(angles), -np.sin(angles)]).astype(np.float32)


def screen_kernel(w_hbm, list_ref, amp_hbm, phase_hbm, f_hbm, slot_hbm, pos_hbm, count_hbm,
                  even_hbm, odd_hbm, plan_hbm, even_ref, odd_ref, w_ref, count_ref, slot_ref, pos_ref,
                  plan_ref, f_ref, amp_ref, phase_ref, weight, parts, halves, kernels, sems):
    small = [pltpu.make_async_copy(w_hbm, w_ref, sems.at[0]),
             pltpu.make_async_copy(f_hbm, f_ref, sems.at[1]),
             pltpu.make_async_copy(slot_hbm, slot_ref, sems.at[12]),
             pltpu.make_async_copy(pos_hbm, pos_ref, sems.at[13]),
             pltpu.make_async_copy(count_hbm, count_ref, sems.at[14])]
    loads = [(pltpu.make_async_copy(phase_hbm.at[s], phase_ref.at[s], sems.at[2 + 2 * s]),
              pltpu.make_async_copy(amp_hbm.at[s], amp_ref.at[s], sems.at[3 + 2 * s]))
             for s in range(SCREENS_DEV)]
    for copy in small + [c for pair in loads for c in pair]:
        copy.start()
    for copy in small:
        copy.wait()
    coords = (lax.broadcasted_iota(jnp.int32, (1, SCREEN), 1) - SCREEN // 2).astype(jnp.float32)
    square = coords * coords * (1.0 / (SCREEN * SCREEN))
    for p in range(PLANES):
        turns = square * w_ref[p]
        turns = turns - jnp.floor(turns + 0.5)
        sin_p, cos_p = sincos(turns * (2.0 * math.pi))
        f_re, f_im = f_ref[0], f_ref[1]
        w_re = (f_re * cos_p - f_im * sin_p).astype(jnp.bfloat16)
        w_im = (f_re * sin_p + f_im * cos_p).astype(jnp.bfloat16)
        top = slice(p * 2 * KSIZE, p * 2 * KSIZE + KSIZE)
        low = slice(p * 2 * KSIZE + KSIZE, (p + 1) * 2 * KSIZE)
        weight[top, :SCREEN] = w_re
        weight[top, SCREEN:] = -w_im
        weight[low, :SCREEN] = w_im
        weight[low, SCREEN:] = w_re
    rows = 32
    for s in range(SCREENS_DEV):
        for copy in loads[s]:
            copy.wait()

        def fill(i, carry):
            at = pl.ds(pl.multiple_of(i * rows, rows), rows)
            sin_v, cos_v = sincos(phase_ref[s, at, :].astype(jnp.float32))
            amp = amp_ref[s, at, :].astype(jnp.float32)
            parts[s % 2, at, :] = (amp * cos_v).astype(jnp.bfloat16)
            parts[s % 2, pl.ds(pl.multiple_of(SCREEN + i * rows, rows), rows), :] = (
                amp * sin_v).astype(jnp.bfloat16)
            return carry
        lax.fori_loop(0, SCREEN // rows, fill, 0)
        for p in range(PLANES):
            half = jnp.dot(weight[p * 128:(p + 1) * 128, :], parts[s % 2],
                           preferred_element_type=jnp.float32).astype(jnp.bfloat16)
            halves[p, s * KSIZE:(s + 1) * KSIZE, :SCREEN] = half[:KSIZE]
            halves[p, s * KSIZE:(s + 1) * KSIZE, SCREEN:] = half[KSIZE:]
    for p in range(PLANES):
        out = lax.dot_general(halves[p], weight[p * 128:(p + 1) * 128, :],
                              (((1,), (1,)), ((), ())), preferred_element_type=jnp.float32)
        out = (out * (1.0 / SCREEN)).astype(jnp.bfloat16)
        for s in range(SCREENS_DEV):
            kernels[s * PLANES + p] = out[s * KSIZE:(s + 1) * KSIZE]

    outs = [pltpu.make_async_copy(plan_ref, plan_hbm, sems.at[15])]
    plan_ref[...] = plan_blocks(slot_ref[...], pos_ref[...], count_ref[0])
    outs[0].start()
    for c, (slots, out) in enumerate([(even_ref, even_hbm), (odd_ref, odd_hbm)]):
        def deliver(t, carry):
            slots[t] = kernels[list_ref[c, t]]
            return carry
        lax.fori_loop(0, OWNERS, deliver, 0)
        outs.append(pltpu.make_async_copy(slots, out, sems.at[10 + c]))
        outs[-1].start()
    for copy in outs:
        copy.wait()


def make_outgoing(depths, send_list, amp, phase, block_slot, block_pos, block_count):
    smem = pl.BlockSpec(memory_space=pltpu.SMEM)
    hbm = pl.BlockSpec(memory_space=pltpu.MemorySpace.HBM)
    slots = jax.ShapeDtypeStruct((OWNERS, KSIZE, 2 * KSIZE), jnp.bfloat16)
    return pl.pallas_call(
        screen_kernel,
        out_shape=(slots, slots, jax.ShapeDtypeStruct((16, 128), jnp.int32)),
        in_specs=[hbm, smem] + [hbm] * 6,
        out_specs=(hbm,) * 3,
        scratch_shapes=[
            pltpu.VMEM(slots.shape, slots.dtype),
            pltpu.VMEM(slots.shape, slots.dtype),
            pltpu.SMEM((PLANES,), jnp.float32),
            pltpu.SMEM((1,), jnp.int32),
            pltpu.VMEM((3, 128), jnp.int32),
            pltpu.VMEM((3, 128), jnp.int32),
            pltpu.VMEM((16, 128), jnp.int32),
            pltpu.VMEM((2, KSIZE, SCREEN), jnp.float32),
            pltpu.VMEM((SCREENS_DEV, SCREEN, SCREEN), jnp.bfloat16),
            pltpu.VMEM((SCREENS_DEV, SCREEN, SCREEN), jnp.bfloat16),
            pltpu.VMEM((PLANES * 128, 2 * SCREEN), jnp.bfloat16),
            pltpu.VMEM((2, 2 * SCREEN, SCREEN), jnp.bfloat16),
            pltpu.VMEM((PLANES, SCREENS_DEV * KSIZE, 2 * SCREEN), jnp.bfloat16),
            pltpu.VMEM((SCREENS_DEV * PLANES, KSIZE, 2 * KSIZE), jnp.bfloat16),
            pltpu.SemaphoreType.DMA((16,)),
        ],
        cost_estimate=pl.CostEstimate(flops=2_700_000_000, bytes_accessed=8_600_000,
                                      transcendentals=2_000_000),
        name="screens",
    )(depths, send_list[0].T, amp, phase, jnp.asarray(dft_rows()), block_slot.reshape(3, 128),
      block_pos.reshape(3, 128), block_count)


def iota(shape, dim):
    return lax.broadcasted_iota(jnp.int32, shape, dim)


def plan_blocks(slot, pos, count):
    bins_total = 2 * POSITIONS
    slot, pos = (jnp.concatenate([v[r:r + 1] for r in range(3)], axis=1) for v in (slot, pos))
    ids = iota((1, BLOCKS_DEV), 1)
    parity = slot & 1
    used = ids < count
    bins = jnp.where(used, parity * POSITIONS + pos, -1)
    hot = (iota((bins_total, BLOCKS_DEV), 0) == bins).astype(jnp.float32)
    upto = (iota((BLOCKS_DEV, BLOCKS_DEV), 0) <= iota((BLOCKS_DEV, BLOCKS_DEV), 1)).astype(jnp.float32)
    count_to = jnp.dot(hot.astype(jnp.bfloat16), upto.astype(jnp.bfloat16),
                       preferred_element_type=jnp.float32)
    rank = jnp.sum(count_to * hot, axis=0, keepdims=True) - 1.0
    groups = jnp.floor((jnp.sum(hot, axis=1, keepdims=True) + (GROUP - 1.0)) * (1.0 / GROUP))
    wide = jnp.broadcast_to(groups, (bins_total, 128))
    b_row, b_col = iota((bins_total, bins_total), 0), iota((bins_total, bins_total), 1)
    earlier = ((b_col < b_row) & ((b_col >= POSITIONS) == (b_row >= POSITIONS))).astype(jnp.float32)
    first = jnp.dot(earlier.astype(jnp.bfloat16), wide.astype(jnp.bfloat16),
                    preferred_element_type=jnp.float32)
    last = first + wide
    place = jnp.sum(hot * first[:, :1], axis=0, keepdims=True) * GROUP + rank
    place = jnp.where(used, place.astype(jnp.int32) + parity * (MAX_GROUPS * GROUP), -1)
    high = (iota((8, BLOCKS_DEV), 0) == (place >> 7)).astype(jnp.float32)
    low = (iota((128, BLOCKS_DEV), 0) == (place & 127)).astype(jnp.float32)
    parts = [(slot >> 1).astype(jnp.float32), (ids & 127).astype(jnp.float32),
             ((ids >> 7) + 1).astype(jnp.float32)]
    spread = lax.dot_general(
        jnp.concatenate([high * part for part in parts], axis=0).astype(jnp.bfloat16),
        low.astype(jnp.bfloat16), (((1,), (1,)), ((), ())), preferred_element_type=jnp.float32)
    owner, block_low, block_high = spread[:8], spread[8:16], spread[16:]
    codes = jnp.where(block_high > 0.0,
                      ((block_high - 1.0) * 128.0 + block_low) * OWNERS + owner + 1.0, 0.0)
    lanes = iota((bins_total, 128), 1)
    past = (last <= lanes.astype(jnp.float32)).astype(jnp.float32)
    onto = (iota((bins_total, 128), 0) == lanes).astype(jnp.float32)
    rows = [codes, jnp.sum(past[:POSITIONS], axis=0, keepdims=True),
            jnp.sum(past[POSITIONS:], axis=0, keepdims=True),
            jnp.sum(onto * last, axis=0, keepdims=True),
            jnp.sum(onto * wide, axis=0, keepdims=True),
            jnp.sum(wide[:POSITIONS], axis=0, keepdims=True),
            jnp.sum(wide[POSITIONS:], axis=0, keepdims=True),
            jnp.zeros((2, 128), jnp.float32)]
    return jnp.concatenate(rows, axis=0).astype(jnp.int32)


ANCHOR_ROW, END_ROW, GROUPS_ROW, TOTAL_ROW = 8, 10, 11, 12


def entry_code(plan, parity, g, i):
    return plan[parity * 4 + (g >> 5), (g & 31) * GROUP + i]


def lanes_low(shape):
    return lax.broadcasted_iota(jnp.int32, shape, len(shape) - 1) < KSIZE


def operator_pair(first, second):
    zero = jnp.zeros((KSIZE, 2 * KSIZE), jnp.bfloat16)
    low = lanes_low((KSIZE, 2 * KSIZE))
    turned = [jnp.concatenate([v[:, KSIZE:], v[:, :KSIZE]], axis=1) for v in (first, second)]
    left = jnp.concatenate([
        jnp.where(low, first, zero), jnp.where(low, -turned[0], zero),
        jnp.where(low, zero, turned[1]), jnp.where(low, zero, -second)], axis=0)
    right = jnp.concatenate([
        jnp.where(low, turned[0], zero), jnp.where(low, first, zero),
        jnp.where(low, zero, second), jnp.where(low, zero, turned[1])], axis=0)
    return jnp.concatenate([left, right], axis=1)


def mix_group(plan, parity, g, recv, left_of, mixed):
    for pair in range(GROUP // 2):
        picked, rows = [], []
        for i in (2 * pair, 2 * pair + 1):
            code = entry_code(plan, parity, g, i)
            place = jnp.maximum(code - 1, 0)
            k = recv[place & (OWNERS - 1)]
            picked.append(jnp.where(code > 0, k, jnp.zeros_like(k)))
            rows.append(left_of(i, place >> 7))
        value = jnp.dot(jnp.concatenate(rows, axis=1), operator_pair(*picked),
                        preferred_element_type=jnp.float32).astype(jnp.bfloat16)
        cols = slice(pair * PATCH, (pair + 1) * PATCH)
        mixed[:PATCH, cols] = value[:, :PATCH]
        mixed[PATCH:, cols] = value[:, PATCH:]


def send_order():
    chips = [(x, y, z) for x in range(4) for y in range(4) for z in range(4)][1:]
    random.Random(0).shuffle(chips)
    order = []
    for chip in chips:
        back = tuple(-d % 4 for d in chip)
        for way in dict.fromkeys((chip, back)):
            if way + (0,) not in order:
                order += [way + (0,), way + (1,)]
    return order + [(0, 0, 0, 1)]


RING = 4
UNROLL = 2
STEPS = MAX_GROUPS // UNROLL + 1


def exchange_kernel(plan, even_hbm, odd_hbm, left_hbm, right_hbm, odd_out, sums_hbm,
                    recv, left, right, mixed, sums, local_sems, send_sems, recv_sems, ring_sems):
    tu, tv = lax.axis_index("tu"), lax.axis_index("tv")
    me = tu * 8 + tv
    x, z, y, core = tu // 4, tu % 4, tv // 2, tv % 2
    for source, target, c in ((even_hbm, recv, 0), (odd_hbm, odd_out, 1)):
        for dx, dy, dz, dc in send_order():
            to_u = (x + dx) % 4 * 4 + (z + dz) % 4
            to_v = (y + dy) % 4 * 2 + (core + dc) % 2
            pltpu.make_async_remote_copy(
                source.at[to_u * 8 + to_v], target.at[me], send_sems.at[c], recv_sems.at[c],
                device_id=(to_u, to_v), device_id_type=pl.DeviceIdType.MESH).start()
    own = [pltpu.make_async_copy(even_hbm.at[me], recv.at[me], local_sems.at[0]),
           pltpu.make_async_copy(odd_hbm.at[me], odd_out.at[me], local_sems.at[1]),
           pltpu.make_async_copy(left_hbm, left, local_sems.at[2]),
           pltpu.make_async_copy(right_hbm, right, local_sems.at[3])]
    for copy in own:
        copy.start()
    mixed[...] = jnp.zeros_like(mixed)
    sums[...] = jnp.zeros_like(sums)
    for copy in own:
        copy.wait()
    others = pl.ds(0, OWNERS - 1)
    pltpu.make_async_copy(recv.at[others], recv.at[others], recv_sems.at[0]).wait()

    def entry(h):
        slot = lax.rem(h, RING)
        return pltpu.make_async_copy(sums.at[slot], sums_hbm.at[h], ring_sems.at[slot])

    def step(h, carry):
        @pl.when(h >= RING)
        def _():
            entry(h - RING).wait()
        slot = lax.rem(h, RING)
        patches = []
        for k in range(UNROLL):
            g = jnp.maximum((h - 1) * UNROLL + k, 0)
            blocks = [jnp.maximum(entry_code(plan, 0, g, i) - 1, 0) >> 7 for i in range(GROUP)]
            weights = jnp.concatenate([right[block] for block in blocks], axis=0)
            patches.append(jnp.dot(mixed[k], weights, preferred_element_type=jnp.float32))
        for k in range(UNROLL):
            g = jnp.minimum(h * UNROLL + k, MAX_GROUPS - 1)
            mix_group(plan, 0, g, recv, lambda i, block: left[block], mixed.at[k])
        prior = sums[lax.rem(h + RING - 1, RING), UNROLL - 1]
        for k in range(UNROLL):
            g = jnp.maximum((h - 1) * UNROLL + k, 0)
            same = plan[ANCHOR_ROW, g] == plan[ANCHOR_ROW, jnp.maximum(g - 1, 0)]
            prior = patches[k] + jnp.where(same, prior, jnp.zeros_like(prior))
            sums[slot, k] = prior
        entry(h).start()
        return carry
    lax.fori_loop(0, STEPS, step, 0)
    for h in range(STEPS - RING, STEPS):
        entry(h).wait()
    for c, source, target in ((0, even_hbm, recv), (1, odd_hbm, odd_out)):
        if c:
            pltpu.make_async_copy(target.at[others], target.at[others], recv_sems.at[c]).wait()
        pltpu.make_async_copy(source.at[others], source.at[others], send_sems.at[c]).wait()


def exchange(plan, even, odd, left, right):
    smem = pl.BlockSpec(memory_space=pltpu.SMEM)
    hbm = pl.BlockSpec(memory_space=pltpu.MemorySpace.HBM)
    return pl.pallas_call(
        exchange_kernel,
        out_shape=(jax.ShapeDtypeStruct(odd.shape, odd.dtype),
                   jax.ShapeDtypeStruct((STEPS, UNROLL, 2 * PATCH, PATCH), jnp.float32)),
        in_specs=[smem, hbm, hbm, hbm, hbm],
        out_specs=(hbm, hbm),
        scratch_shapes=[
            pltpu.VMEM(even.shape, even.dtype),
            pltpu.VMEM(left.shape, left.dtype),
            pltpu.VMEM(right.shape, right.dtype),
            pltpu.VMEM((UNROLL, 2 * PATCH, GROUP * KSIZE), jnp.bfloat16),
            pltpu.VMEM((RING, UNROLL, 2 * PATCH, PATCH), jnp.float32),
            pltpu.SemaphoreType.DMA((4,)),
            pltpu.SemaphoreType.DMA((2,)),
            pltpu.SemaphoreType.DMA((2,)),
            pltpu.SemaphoreType.DMA((RING,)),
        ],
        compiler_params=pltpu.CompilerParams(has_side_effects=True),
        name="exchange",
    )(plan, even, odd, left, right)


def turn(v):
    return pltpu.roll(v, KSIZE, 1)


def finish_kernel(plan, recv_hbm, left_hbm, right_hbm, sums_hbm, main, bottom, side,
                  recv, grid, mixed, lbuf, rbuf, sums, sems, misc_sems):
    steps = (plan[TOTAL_ROW + 1, 0] + UNROLL - 1) // UNROLL
    received = pltpu.make_async_copy(recv_hbm, recv, misc_sems.at[0])
    received.start()

    def start(h):
        slot = lax.rem(h, DEPTH)
        for k in range(UNROLL):
            for i in range(GROUP):
                block = jnp.maximum(entry_code(plan, 1, h * UNROLL + k, i) - 1, 0) >> 7
                n = k * GROUP + i
                pltpu.make_async_copy(left_hbm.at[block], lbuf.at[slot, n], sems.at[0, slot]).start()
                pltpu.make_async_copy(right_hbm.at[block], rbuf.at[slot, n], sems.at[1, slot]).start()

    for h in range(DEPTH - 2):
        @pl.when(h < steps)
        def _():
            start(h)

    def even_sum(q):
        at = plan[END_ROW, q] - 1 + UNROLL
        return pltpu.make_async_copy(sums_hbm.at[at // UNROLL, lax.rem(at, UNROLL)], sums.at[q],
                                     misc_sems.at[1 + q])

    def start_sum(q, carry):
        @pl.when(plan[GROUPS_ROW, q] > 0)
        def _():
            even_sum(q).start()
        return carry
    lax.fori_loop(0, POSITIONS, start_sum, 0)
    grid[...] = jnp.zeros_like(grid)
    mixed[...] = jnp.zeros_like(mixed)
    rbuf[DEPTH - 1] = jnp.zeros_like(rbuf[0])
    received.wait()

    def add(anchor, patch):
        row = pl.ds(pl.multiple_of((anchor >> 3) * KSIZE, KSIZE), PATCH)
        odd, col = anchor & 1, (anchor & 7) >> 1
        grid[odd, col, 0, row, :] += patch[:PATCH]
        grid[odd, col, 1, row, :] += patch[PATCH:]

    def step(h, carry):
        slot = lax.rem(h, DEPTH)

        @pl.when(h + DEPTH - 2 < steps)
        def _():
            start(h + DEPTH - 2)

        @pl.when(h < steps)
        def _():
            pltpu.make_async_copy(lbuf.at[slot], lbuf.at[slot], sems.at[0, slot]).wait()
            pltpu.make_async_copy(rbuf.at[slot], rbuf.at[slot], sems.at[1, slot]).wait()
        earlier = lax.rem(h + DEPTH - 1, DEPTH)
        patches = []
        for k in range(UNROLL):
            weights = jnp.concatenate([rbuf[earlier, k * GROUP + i] for i in range(GROUP)], axis=0)
            patches.append(jnp.dot(mixed[k], weights, preferred_element_type=jnp.float32))
        for k in range(UNROLL):
            g = jnp.minimum(h * UNROLL + k, MAX_GROUPS - 1)
            mix_group(plan, 1, g, recv, lambda i, block: lbuf[slot, k * GROUP + i], mixed.at[k])
        for k in range(UNROLL):
            g = jnp.maximum((h - 1) * UNROLL + k, 0)
            add(jnp.minimum(plan[ANCHOR_ROW + 1, g], POSITIONS - 1), patches[k])
        return carry

    @pl.when(steps > 0)
    def _():
        lax.fori_loop(0, steps + 1, step, 0)

    def add_sum(q, carry):
        @pl.when(plan[GROUPS_ROW, q] > 0)
        def _():
            even_sum(q).wait()
            add(q, sums[q])
        return carry
    lax.fori_loop(0, POSITIONS, add_sum, 0)
    low = lanes_low((KSIZE, PATCH))
    for plane in range(2):
        for r in range(EXT_U // KSIZE):
            rows = slice(r * KSIZE, (r + 1) * KSIZE)
            shifted = [turn(grid[1, col, plane, rows, :]) for col in range(4)]
            for col in range(4):
                before = shifted[col - 1] if col else jnp.zeros_like(shifted[0])
                value = grid[0, col, plane, rows, :] + jnp.where(low, before, shifted[col])
                cols = slice(col * PATCH, (col + 1) * PATCH)
                if r < TILE_U // KSIZE:
                    main[plane, rows, cols] = value
                else:
                    bottom[plane, :, cols] = value.astype(jnp.bfloat16)
    for r in range(EXT_U // KSIZE):
        rows = slice(r * KSIZE, (r + 1) * KSIZE)
        value = jnp.where(low, turn(grid[1, 3, 0, rows, :]), grid[1, 3, 1, rows, :])
        side[rows, :] = value.astype(jnp.bfloat16)


GRID_SHAPE = (2, 4, 2, EXT_U, PATCH)


def finish(plan, recv, left, right, sums):
    vmem = pl.BlockSpec(memory_space=pltpu.VMEM)
    smem = pl.BlockSpec(memory_space=pltpu.SMEM)
    hbm = pl.BlockSpec(memory_space=pltpu.MemorySpace.HBM)
    return pl.pallas_call(
        finish_kernel,
        out_shape=(jax.ShapeDtypeStruct((2, TILE_U, TILE_V), jnp.float32),
                   jax.ShapeDtypeStruct((2, KSIZE, TILE_V), jnp.bfloat16),
                   jax.ShapeDtypeStruct((EXT_U, PATCH), jnp.bfloat16)),
        in_specs=[smem] + [hbm] * 4,
        out_specs=(vmem, vmem, vmem),
        scratch_shapes=[
            pltpu.VMEM(recv.shape, recv.dtype),
            pltpu.VMEM(GRID_SHAPE, jnp.float32),
            pltpu.VMEM((UNROLL, 2 * PATCH, GROUP * KSIZE), jnp.bfloat16),
            pltpu.VMEM((DEPTH, UNROLL * GROUP, PATCH, 2 * KSIZE), jnp.bfloat16),
            pltpu.VMEM((DEPTH, UNROLL * GROUP, KSIZE, PATCH), jnp.bfloat16),
            pltpu.VMEM((POSITIONS, 2 * PATCH, PATCH), jnp.float32),
            pltpu.SemaphoreType.DMA((2, DEPTH)),
            pltpu.SemaphoreType.DMA((1 + POSITIONS,)),
        ],
        cost_estimate=pl.CostEstimate(flops=1_000_000_000, bytes_accessed=12_000_000,
                                      transcendentals=0),
        name="finish",
    )(plan, recv, left, right, sums)


def border_kernel(bottom, side, bottom_out, side_out, corner_out, send_sems, recv_sems):
    tu, tv = lax.axis_index("tu"), lax.axis_index("tv")
    n_tu, n_tv = lax.axis_size("tu"), lax.axis_size("tv")
    ways = ((1, 0), (0, 1), (1, 1))
    barrier = pltpu.get_barrier_semaphore()
    for du, dv in ways:
        for sign in (1, -1):
            other = ((tu + n_tu + sign * du) % n_tu, (tv + n_tv + sign * dv) % n_tv)
            pl.semaphore_signal(barrier, inc=1, device_id=other, device_id_type=pl.DeviceIdType.MESH)
    pl.semaphore_wait(barrier, 2 * len(ways))
    parts = ((bottom, bottom_out), (side.at[pl.ds(0, TILE_U)], side_out),
             (side.at[pl.ds(TILE_U, KSIZE)], corner_out))
    copies = []
    for n, ((du, dv), (source, target)) in enumerate(zip(ways, parts)):
        copies.append(pltpu.make_async_remote_copy(
            source, target, send_sems.at[n], recv_sems.at[n],
            device_id=((tu + du) % n_tu, (tv + dv) % n_tv), device_id_type=pl.DeviceIdType.MESH))
        copies[-1].start()
    for copy in copies:
        copy.wait()


def borders(bottom, side):
    hbm = pl.BlockSpec(memory_space=pltpu.MemorySpace.HBM)
    return pl.pallas_call(
        border_kernel,
        out_shape=(jax.ShapeDtypeStruct(bottom.shape, bottom.dtype),
                   jax.ShapeDtypeStruct((TILE_U, PATCH), side.dtype),
                   jax.ShapeDtypeStruct((KSIZE, PATCH), side.dtype)),
        in_specs=[hbm, hbm],
        out_specs=(hbm,) * 3,
        scratch_shapes=[pltpu.SemaphoreType.DMA((3,)), pltpu.SemaphoreType.DMA((3,))],
        compiler_params=pltpu.CompilerParams(collective_id=1, has_side_effects=True),
        name="borders",
    )(bottom, side)


def join_kernel(main, bottom_hbm, side_hbm, corner_hbm, out, top, left, bottom, side, corner, sems):
    strips = [(top, (slice(None), pl.ds(0, KSIZE))),
              (left, (slice(None), pl.ds(KSIZE, TILE_U - KSIZE), pl.ds(0, PATCH)))]
    loads = [pltpu.make_async_copy(main.at[at], strip, sems.at[n]) for n, (strip, at) in enumerate(strips)]
    loads += [pltpu.make_async_copy(bottom_hbm, bottom, sems.at[2]),
              pltpu.make_async_copy(side_hbm, side, sems.at[3]),
              pltpu.make_async_copy(corner_hbm, corner, sems.at[4])]
    for copy in loads:
        copy.start()
    for copy in loads:
        copy.wait()
    above, beside = lax.axis_index("tu") > 0, lax.axis_index("tv") > 0

    def kept(flag, value):
        value = value.astype(jnp.float32)
        return jnp.where(flag, value, jnp.zeros_like(value))
    top[...] += kept(above, bottom[...])
    edge = kept(beside, side[...])
    tip = kept(above & beside, corner[...]) + edge[:KSIZE]
    low = lanes_low((KSIZE, PATCH))
    zero = jnp.zeros((KSIZE, PATCH), jnp.float32)
    top[0, :, :PATCH] += jnp.where(low, tip, zero)
    top[1, :, :PATCH] += jnp.where(low, turn(tip), zero)
    for r in range(1, TILE_U // KSIZE):
        rows = slice((r - 1) * KSIZE, r * KSIZE)
        part = edge[r * KSIZE:(r + 1) * KSIZE]
        left[0, rows, :] += jnp.where(low, part, zero)
        left[1, rows, :] += jnp.where(low, turn(part), zero)
    stores = [pltpu.make_async_copy(strip, out.at[at], sems.at[5 + n]) for n, (strip, at) in enumerate(strips)]
    for copy in stores:
        copy.start()
    for copy in stores:
        copy.wait()


def join(main, bottom, side, corner):
    hbm = pl.BlockSpec(memory_space=pltpu.MemorySpace.HBM)
    return pl.pallas_call(
        join_kernel,
        out_shape=jax.ShapeDtypeStruct(main.shape, main.dtype),
        in_specs=[hbm] * 4,
        out_specs=hbm,
        input_output_aliases={0: 0},
        scratch_shapes=[
            pltpu.VMEM((2, KSIZE, TILE_V), jnp.float32),
            pltpu.VMEM((2, TILE_U - KSIZE, PATCH), jnp.float32),
            pltpu.VMEM(bottom.shape, bottom.dtype),
            pltpu.VMEM(side.shape, side.dtype),
            pltpu.VMEM(corner.shape, corner.dtype),
            pltpu.SemaphoreType.DMA((7,)),
        ],
        name="join_borders",
    )(main, bottom, side, corner)


def shards(aperture_amp, aperture_phase, plane_depths, send_list, send_count, vis_left, vis_right,
           block_slot, block_pos, block_count):
    even, odd, plan = make_outgoing(plane_depths, send_list, aperture_amp, aperture_phase,
                                    block_slot, block_pos, block_count)
    recv, sums = exchange(plan, even, odd, vis_left, vis_right)
    main, bottom, side = finish(plan, recv, vis_left, vis_right, sums)
    return join(main, *borders(bottom, side))


def solution(mesh):
    placed = (
        P(("tu", "tv"), None, None),
        P(("tu", "tv"), None, None),
        P(),
        P(("tu", "tv"), None, None),
        P(("tu", "tv"), None),
        P(("tu", "tv"), None, None),
        P(("tu", "tv"), None, None),
        P(("tu", "tv")),
        P(("tu", "tv")),
        P(("tu", "tv")),
    )
    return jax.shard_map(
        shards, mesh=mesh, in_specs=placed, out_specs=P(None, "tu", "tv"), check_vma=False
    )
```

profile of v0, /device:TPU:0, one launch (start us, length us, event | category | flops | bytes accessed | tf_op | source)
XLA Modules:
  0.0 110.8 jit_solution(1836347207760668938)
XLA Ops:
  0.7 13.2 %screens.1 = (bf16[128,64,128]{2,1,0:T(8,128)(2,1)}, bf16[128,64,128]{2,1,0:T(8,128)(2,1)}, s32[16,128]{1,0:T(8,128)}) custom-call(f32[4]{0:T(128)} %w_hbm.1, s32[2,128]{1,0:T(2,128)} %bitcast.7, bf16[4,512,512]{2,1,0:T(8,128)(2,1)} %amp_hbm.1, bf16[4,512,512]{2,1,0:T(8,128)(2,1)} %phase_hbm.1, f32[2,64,512]{2,1,0:T(8,128)} %constant.2.clone.f_hbm, ...), custom_call_target="tpu_custom_call" | custom-call | flops 2700000000 | bytes 8600000 | tf_op jit(solution)/shard_map/screens/pallas_call | solution.py:125
  13.8 70.8 %exchange.1 = (bf16[128,64,128]{2,1,0:T(8,128)(2,1)}, f32[65,2,256,128]{3,2,1,0:T(8,128)}) custom-call(s32[16,128]{1,0:T(8,128)} %get-tuple-element.16.plan, bf16[128,64,128]{2,1,0:T(8,128)(2,1)} %get-tuple-element.17.even_hbm, bf16[128,64,128]{2,1,0:T(8,128)(2,1)} %get-tuple-element.18.odd_hbm, bf16[384,128,128]{2,1,0:T(8,128)(2,1)} %left_hbm.3, ...), custom_call_target="tpu_custom_call" | custom-call | tf_op jit(solution)/shard_map/exchange/pallas_call | solution.py:322
  84.7 12.0 %finish.1 = (f32[2,256,512]{2,1,0:T(8,128)}, bf16[2,64,512]{2,1,0:T(8,128)(2,1)}, bf16[320,128]{1,0:T(8,128)(2,1)}) custom-call(s32[16,128]{1,0:T(8,128)} %get-tuple-element.16.plan, bf16[128,64,128]{2,1,0:T(8,128)(2,1)} %get-tuple-element.19.recv_hbm, bf16[384,128,128]{2,1,0:T(8,128)(2,1)} %left_hbm.3, bf16[384,64,128]{2,1,0:T(8,128)(2,1)} %right_hbm.3, ...), custom_call_target="tpu_custom_call" | custom-call | flops 1000000000 | bytes 12000000 | tf_op jit(solution)/shard_map/finish/pallas_call | solution.py:451
  96.7 12.1 %borders.1 = (bf16[2,64,512]{2,1,0:T(8,128)(2,1)}, bf16[256,128]{1,0:T(8,128)(2,1)}, bf16[64,128]{1,0:T(8,128)(2,1)}) custom-call(bf16[2,64,512]{2,1,0:T(8,128)(2,1)} %get-tuple-element.22.bottom, bf16[320,128]{1,0:T(8,128)(2,1)} %get-tuple-element.23.side), custom_call_target="tpu_custom_call" | custom-call | tf_op jit(solution)/shard_map/borders/pallas_call | solution.py:498
  108.8 2.0 %join_borders.1 = f32[2,256,512]{2,1,0:T(8,128)} custom-call(f32[2,256,512]{2,1,0:T(8,128)} %get-tuple-element.21.main, bf16[2,64,512]{2,1,0:T(8,128)(2,1)} %get-tuple-element.24.bottom_hbm, bf16[256,128]{1,0:T(8,128)(2,1)} %get-tuple-element.25.side_hbm, bf16[64,128]{1,0:T(8,128)(2,1)} %get-tuple-element.26.corner_hbm), custom_call_target="tpu_custom_call", output_to_operand_aliasing={{}: (0, {})} | custom-call | tf_op jit(solution)/shard_map/join_borders/pallas_call | solution.py:548
where the time goes:
time: 113 us; the launch traced here: 111 us
  Pallas kernels  110 us (97%)
    pallas_call x1, Pallas kernels, exchange(): pl.pallas_call(exchange_kernel, out_shape=(jax.ShapeDtypeStruct(odd.shape...  70.8 us
    pallas_call x1, Pallas kernels, make_outgoing(): pl.pallas_call(screen_kernel, out_shape=(slots, slots, jax.ShapeDtypeStru...  13.2 us
    pallas_call x1, Pallas kernels, borders(): pl.pallas_call(border_kernel, out_shape=(jax.ShapeDtypeStruct(bottom.shap...  12.1 us
    pallas_call x1, Pallas kernels, finish(): pl.pallas_call(finish_kernel, out_shape=(jax.ShapeDtypeStruct((2, TILE_U,...  12 us

commit v1 on v0

--- a/solution.py
+++ b/solution.py
@@ -41,6 +41,24 @@
     return s * x, k
 
 
+HALF_SIN = (0.7071043848991394, -0.029459532350301743, 0.0003670911828521639, -2.0289162421249785e-06)
+HALF_COS = (1.4142135381698608, -0.17677636444568634, 0.003682575421407819, -3.061264942516573e-05,
+            1.279086063732393e-07)
+
+
+def polar(amp, x):
+    z = x * x
+    s = jnp.float32(HALF_SIN[-1])
+    for c in HALF_SIN[-2::-1]:
+        s = s * z + c
+    s = s * x
+    k = jnp.float32(HALF_COS[-1])
+    for c in HALF_COS[-2::-1]:
+        k = k * z + c
+    scaled = amp * s
+    return amp - scaled * s, scaled * k
+
+
 def dft_rows():
     freq = np.arange(KSIZE) - KSIZE // 2
     turns = np.mod(freq[:, None] * np.arange(SCREEN)[None, :], SCREEN)
@@ -50,7 +68,7 @@
 
 def screen_kernel(w_hbm, list_ref, amp_hbm, phase_hbm, f_hbm, slot_hbm, pos_hbm, count_hbm,
                   even_hbm, odd_hbm, plan_hbm, even_ref, odd_ref, w_ref, count_ref, slot_ref, pos_ref,
-                  plan_ref, f_ref, amp_ref, phase_ref, weight, parts, halves, kernels, sems):
+                  plan_ref, f_ref, amp_ref, phase_ref, weight, parts_a, parts_b, halves, kernels, sems):
     small = [pltpu.make_async_copy(w_hbm, w_ref, sems.at[0]),
              pltpu.make_async_copy(f_hbm, f_ref, sems.at[1]),
              pltpu.make_async_copy(slot_hbm, slot_ref, sems.at[12]),
@@ -78,25 +96,30 @@
         weight[top, SCREEN:] = -w_im
         weight[low, :SCREEN] = w_im
         weight[low, SCREEN:] = w_re
-    rows = 32
-    for s in range(SCREENS_DEV):
-        for copy in loads[s]:
-            copy.wait()
-
-        def fill(i, carry):
-            at = pl.ds(pl.multiple_of(i * rows, rows), rows)
-            sin_v, cos_v = sincos(phase_ref[s, at, :].astype(jnp.float32))
-            amp = amp_ref[s, at, :].astype(jnp.float32)
-            parts[s % 2, at, :] = (amp * cos_v).astype(jnp.bfloat16)
-            parts[s % 2, pl.ds(pl.multiple_of(SCREEN + i * rows, rows), rows), :] = (
-                amp * sin_v).astype(jnp.bfloat16)
+    rows = 16
+    parts = (parts_a, parts_b)
+    for s in range(SCREENS_DEV + 1):
+        if s < SCREENS_DEV:
+            for copy in loads[s]:
+                copy.wait()
+
+        def part(p, carry):
+            if s > 0:
+                at = pl.ds(pl.multiple_of(p * 128, 128), 128)
+                half = jnp.dot(weight[at, :], parts[(s - 1) % 2][...], preferred_element_type=jnp.float32)
+                half = half.astype(jnp.bfloat16)
+                kept = slice((s - 1) * KSIZE, s * KSIZE)
+                halves[p, kept, :SCREEN] = half[:KSIZE]
+                halves[p, kept, SCREEN:] = half[KSIZE:]
+            if s < SCREENS_DEV:
+                for i in range(SCREEN // PLANES // rows):
+                    start = pl.multiple_of(p * (SCREEN // PLANES) + i * rows, rows)
+                    at = pl.ds(start, rows)
+                    re, im = polar(amp_ref[s, at, :].astype(jnp.float32), phase_ref[s, at, :].astype(jnp.float32))
+                    parts[s % 2][at, :] = re.astype(jnp.bfloat16)
+                    parts[s % 2][pl.ds(pl.multiple_of(SCREEN + start, rows), rows), :] = im.astype(jnp.bfloat16)
             return carry
-        lax.fori_loop(0, SCREEN // rows, fill, 0)
-        for p in range(PLANES):
-            half = jnp.dot(weight[p * 128:(p + 1) * 128, :], parts[s % 2],
-                           preferred_element_type=jnp.float32).astype(jnp.bfloat16)
-            halves[p, s * KSIZE:(s + 1) * KSIZE, :SCREEN] = half[:KSIZE]
-            halves[p, s * KSIZE:(s + 1) * KSIZE, SCREEN:] = half[KSIZE:]
+        lax.fori_loop(0, PLANES, part, 0)
     for p in range(PLANES):
         out = lax.dot_general(halves[p], weight[p * 128:(p + 1) * 128, :],
                               (((1,), (1,)), ((), ())), preferred_element_type=jnp.float32)
@@ -124,7 +147,7 @@
     slots = jax.ShapeDtypeStruct((OWNERS, KSIZE, 2 * KSIZE), jnp.bfloat16)
     return pl.pallas_call(
         screen_kernel,
-        out_shape=(slots, slots, jax.ShapeDtypeStruct((16, 128), jnp.int32)),
+        out_shape=(slots, slots, jax.ShapeDtypeStruct((PLAN_ROWS, 128), jnp.int32)),
         in_specs=[hbm, smem] + [hbm] * 6,
         out_specs=(hbm,) * 3,
         scratch_shapes=[
@@ -134,12 +157,13 @@
             pltpu.SMEM((1,), jnp.int32),
             pltpu.VMEM((3, 128), jnp.int32),
             pltpu.VMEM((3, 128), jnp.int32),
-            pltpu.VMEM((16, 128), jnp.int32),
+            pltpu.VMEM((PLAN_ROWS, 128), jnp.int32),
             pltpu.VMEM((2, KSIZE, SCREEN), jnp.float32),
             pltpu.VMEM((SCREENS_DEV, SCREEN, SCREEN), jnp.bfloat16),
             pltpu.VMEM((SCREENS_DEV, SCREEN, SCREEN), jnp.bfloat16),
             pltpu.VMEM((PLANES * 128, 2 * SCREEN), jnp.bfloat16),
-            pltpu.VMEM((2, 2 * SCREEN, SCREEN), jnp.bfloat16),
+            pltpu.VMEM((2 * SCREEN, SCREEN), jnp.bfloat16),
+            pltpu.VMEM((2 * SCREEN, SCREEN), jnp.bfloat16),
             pltpu.VMEM((PLANES, SCREENS_DEV * KSIZE, 2 * SCREEN), jnp.bfloat16),
             pltpu.VMEM((SCREENS_DEV * PLANES, KSIZE, 2 * KSIZE), jnp.bfloat16),
             pltpu.SemaphoreType.DMA((16,)),
@@ -184,26 +208,25 @@
         jnp.concatenate([high * part for part in parts], axis=0).astype(jnp.bfloat16),
         low.astype(jnp.bfloat16), (((1,), (1,)), ((), ())), preferred_element_type=jnp.float32)
     owner, block_low, block_high = spread[:8], spread[8:16], spread[16:]
-    codes = jnp.where(block_high > 0.0,
-                      ((block_high - 1.0) * 128.0 + block_low) * OWNERS + owner + 1.0, 0.0)
+    taken = block_high > 0.0
+    owners = jnp.where(taken, owner, float(OWNERS))
+    blocks = jnp.where(taken, (block_high - 1.0) * 128.0 + block_low, 0.0)
     lanes = iota((bins_total, 128), 1)
     past = (last <= lanes.astype(jnp.float32)).astype(jnp.float32)
     onto = (iota((bins_total, 128), 0) == lanes).astype(jnp.float32)
-    rows = [codes, jnp.sum(past[:POSITIONS], axis=0, keepdims=True),
+    rows = [owners, jnp.sum(past[:POSITIONS], axis=0, keepdims=True),
             jnp.sum(past[POSITIONS:], axis=0, keepdims=True),
             jnp.sum(onto * last, axis=0, keepdims=True),
             jnp.sum(onto * wide, axis=0, keepdims=True),
             jnp.sum(wide[:POSITIONS], axis=0, keepdims=True),
             jnp.sum(wide[POSITIONS:], axis=0, keepdims=True),
-            jnp.zeros((2, 128), jnp.float32)]
+            jnp.zeros((2, 128), jnp.float32), blocks]
     return jnp.concatenate(rows, axis=0).astype(jnp.int32)
 
 
-ANCHOR_ROW, END_ROW, GROUPS_ROW, TOTAL_ROW = 8, 10, 11, 12
-
-
-def entry_code(plan, parity, g, i):
-    return plan[parity * 4 + (g >> 5), (g & 31) * GROUP + i]
+PLAN_ROWS = 24
+ANCHORS, ENDS, GROUPS, TOTALS, BLOCKS = (row * 128 for row in (8, 10, 11, 12, 16))
+LIST = MAX_GROUPS * GROUP
 
 
 def lanes_low(shape):
@@ -223,16 +246,10 @@
     return jnp.concatenate([left, right], axis=1)
 
 
-def mix_group(plan, parity, g, recv, left_of, mixed):
+def mix_group(kernels, rows, mixed):
     for pair in range(GROUP // 2):
-        picked, rows = [], []
-        for i in (2 * pair, 2 * pair + 1):
-            code = entry_code(plan, parity, g, i)
-            place = jnp.maximum(code - 1, 0)
-            k = recv[place & (OWNERS - 1)]
-            picked.append(jnp.where(code > 0, k, jnp.zeros_like(k)))
-            rows.append(left_of(i, place >> 7))
-        value = jnp.dot(jnp.concatenate(rows, axis=1), operator_pair(*picked),
+        two = slice(2 * pair, 2 * pair + 2)
+        value = jnp.dot(jnp.concatenate(rows[two], axis=1), operator_pair(*kernels[two]),
                         preferred_element_type=jnp.float32).astype(jnp.bfloat16)
         cols = slice(pair * PATCH, (pair + 1) * PATCH)
         mixed[:PATCH, cols] = value[:, :PATCH]
@@ -252,8 +269,9 @@
 
 
 RING = 4
-UNROLL = 2
+UNROLL = 4
 STEPS = MAX_GROUPS // UNROLL + 1
+PER_STEP = UNROLL * GROUP
 
 
 def exchange_kernel(plan, even_hbm, odd_hbm, left_hbm, right_hbm, odd_out, sums_hbm,
@@ -276,6 +294,7 @@
         copy.start()
     mixed[...] = jnp.zeros_like(mixed)
     sums[...] = jnp.zeros_like(sums)
+    recv[OWNERS] = jnp.zeros_like(recv[OWNERS])
     for copy in own:
         copy.wait()
     others = pl.ds(0, OWNERS - 1)
@@ -290,24 +309,27 @@
         def _():
             entry(h - RING).wait()
         slot = lax.rem(h, RING)
+        before, anchors = carry
+        blocks = [plan[BLOCKS + h * PER_STEP + n] for n in range(PER_STEP)]
+        owners = [plan[h * PER_STEP + n] for n in range(PER_STEP)]
         patches = []
         for k in range(UNROLL):
-            g = jnp.maximum((h - 1) * UNROLL + k, 0)
-            blocks = [jnp.maximum(entry_code(plan, 0, g, i) - 1, 0) >> 7 for i in range(GROUP)]
-            weights = jnp.concatenate([right[block] for block in blocks], axis=0)
+            weights = jnp.concatenate([right[n] for n in before[k * GROUP:(k + 1) * GROUP]], axis=0)
             patches.append(jnp.dot(mixed[k], weights, preferred_element_type=jnp.float32))
         for k in range(UNROLL):
-            g = jnp.minimum(h * UNROLL + k, MAX_GROUPS - 1)
-            mix_group(plan, 0, g, recv, lambda i, block: left[block], mixed.at[k])
-        prior = sums[lax.rem(h + RING - 1, RING), UNROLL - 1]
-        for k in range(UNROLL):
-            g = jnp.maximum((h - 1) * UNROLL + k, 0)
-            same = plan[ANCHOR_ROW, g] == plan[ANCHOR_ROW, jnp.maximum(g - 1, 0)]
-            prior = patches[k] + jnp.where(same, prior, jnp.zeros_like(prior))
-            sums[slot, k] = prior
+            mine = slice(k * GROUP, (k + 1) * GROUP)
+            mix_group([recv[n] for n in owners[mine]], [left[n] for n in blocks[mine]], mixed.at[k])
+        last = lax.rem(h + RING - 1, RING)
+        same = [anchors[k] == anchors[k + 1] for k in range(UNROLL)]
+        for r in range(0, 2 * PATCH, 32):
+            rows = slice(r, r + 32)
+            prior = sums[last, UNROLL - 1, rows]
+            for k in range(UNROLL):
+                prior = patches[k][rows] + jnp.where(same[k], prior, jnp.zeros_like(prior))
+                sums[slot, k, rows] = prior
         entry(h).start()
-        return carry
-    lax.fori_loop(0, STEPS, step, 0)
+        return blocks, [anchors[UNROLL]] + [plan[ANCHORS + h * UNROLL + k] for k in range(UNROLL)]
+    lax.fori_loop(0, STEPS, step, ([jnp.int32(0)] * PER_STEP, [jnp.int32(0)] * (UNROLL + 1)))
     for h in range(STEPS - RING, STEPS):
         entry(h).wait()
     for c, source, target in ((0, even_hbm, recv), (1, odd_hbm, odd_out)):
@@ -326,7 +348,7 @@
         in_specs=[smem, hbm, hbm, hbm, hbm],
         out_specs=(hbm, hbm),
         scratch_shapes=[
-            pltpu.VMEM(even.shape, even.dtype),
+            pltpu.VMEM((OWNERS + 1, *even.shape[1:]), even.dtype),
             pltpu.VMEM(left.shape, left.dtype),
             pltpu.VMEM(right.shape, right.dtype),
             pltpu.VMEM((UNROLL, 2 * PATCH, GROUP * KSIZE), jnp.bfloat16),
@@ -347,18 +369,16 @@
 
 def finish_kernel(plan, recv_hbm, left_hbm, right_hbm, sums_hbm, main, bottom, side,
                   recv, grid, mixed, lbuf, rbuf, sums, sems, misc_sems):
-    steps = (plan[TOTAL_ROW + 1, 0] + UNROLL - 1) // UNROLL
-    received = pltpu.make_async_copy(recv_hbm, recv, misc_sems.at[0])
+    steps = (plan[TOTALS + 128] + UNROLL - 1) // UNROLL
+    received = pltpu.make_async_copy(recv_hbm, recv.at[pl.ds(0, OWNERS)], misc_sems.at[0])
     received.start()
 
     def start(h):
         slot = lax.rem(h, DEPTH)
-        for k in range(UNROLL):
-            for i in range(GROUP):
-                block = jnp.maximum(entry_code(plan, 1, h * UNROLL + k, i) - 1, 0) >> 7
-                n = k * GROUP + i
-                pltpu.make_async_copy(left_hbm.at[block], lbuf.at[slot, n], sems.at[0, slot]).start()
-                pltpu.make_async_copy(right_hbm.at[block], rbuf.at[slot, n], sems.at[1, slot]).start()
+        for n in range(PER_STEP):
+            block = plan[BLOCKS + LIST + h * PER_STEP + n]
+            pltpu.make_async_copy(left_hbm.at[block], lbuf.at[slot, n], sems.at[0, slot]).start()
+            pltpu.make_async_copy(right_hbm.at[block], rbuf.at[slot, n], sems.at[1, slot]).start()
 
     for h in range(DEPTH - 2):
         @pl.when(h < steps)
@@ -366,12 +386,12 @@
             start(h)
 
     def even_sum(q):
-        at = plan[END_ROW, q] - 1 + UNROLL
+        at = plan[ENDS + q] - 1 + UNROLL
         return pltpu.make_async_copy(sums_hbm.at[at // UNROLL, lax.rem(at, UNROLL)], sums.at[q],
                                      misc_sems.at[1 + q])
 
     def start_sum(q, carry):
-        @pl.when(plan[GROUPS_ROW, q] > 0)
+        @pl.when(plan[GROUPS + q] > 0)
         def _():
             even_sum(q).start()
         return carry
@@ -379,6 +399,7 @@
     grid[...] = jnp.zeros_like(grid)
     mixed[...] = jnp.zeros_like(mixed)
     rbuf[DEPTH - 1] = jnp.zeros_like(rbuf[0])
+    recv[OWNERS] = jnp.zeros_like(recv[OWNERS])
     received.wait()
 
     def add(anchor, patch):
@@ -404,19 +425,19 @@
             weights = jnp.concatenate([rbuf[earlier, k * GROUP + i] for i in range(GROUP)], axis=0)
             patches.append(jnp.dot(mixed[k], weights, preferred_element_type=jnp.float32))
         for k in range(UNROLL):
-            g = jnp.minimum(h * UNROLL + k, MAX_GROUPS - 1)
-            mix_group(plan, 1, g, recv, lambda i, block: lbuf[slot, k * GROUP + i], mixed.at[k])
+            mine = range(k * GROUP, (k + 1) * GROUP)
+            mix_group([recv[plan[LIST + h * PER_STEP + n]] for n in mine],
+                      [lbuf[slot, n] for n in mine], mixed.at[k])
         for k in range(UNROLL):
-            g = jnp.maximum((h - 1) * UNROLL + k, 0)
-            add(jnp.minimum(plan[ANCHOR_ROW + 1, g], POSITIONS - 1), patches[k])
-        return carry
+            add(carry[k], patches[k])
+        return [jnp.minimum(plan[ANCHORS + MAX_GROUPS + h * UNROLL + k], POSITIONS - 1) for k in range(UNROLL)]
 
     @pl.when(steps > 0)
     def _():
-        lax.fori_loop(0, steps + 1, step, 0)
+        lax.fori_loop(0, steps + 1, step, [jnp.int32(0)] * UNROLL)
 
     def add_sum(q, carry):
-        @pl.when(plan[GROUPS_ROW, q] > 0)
+        @pl.when(plan[GROUPS + q] > 0)
         def _():
             even_sum(q).wait()
             add(q, sums[q])
@@ -456,7 +477,7 @@
         in_specs=[smem] + [hbm] * 4,
         out_specs=(vmem, vmem, vmem),
         scratch_shapes=[
-            pltpu.VMEM(recv.shape, recv.dtype),
+            pltpu.VMEM((OWNERS + 1, *recv.shape[1:]), recv.dtype),
             pltpu.VMEM(GRID_SHAPE, jnp.float32),
             pltpu.VMEM((UNROLL, 2 * PATCH, GROUP * KSIZE), jnp.bfloat16),
             pltpu.VMEM((DEPTH, UNROLL * GROUP, PATCH, 2 * KSIZE), jnp.bfloat16),
@@ -567,6 +588,7 @@
            block_slot, block_pos, block_count):
     even, odd, plan = make_outgoing(plane_depths, send_list, aperture_amp, aperture_phase,
                                     block_slot, block_pos, block_count)
+    plan = plan.reshape(-1)
     recv, sums = exchange(plan, even, odd, vis_left, vis_right)
     main, bottom, side = finish(plan, recv, vis_left, vis_right, sums)
     return join(main, *borders(bottom, side))

time: 113 us -> 104 us (0.920); the launches traced: 111 us -> 103 us
  Pallas kernels: 110 us -> 102 us
    pallas_call x1, Pallas kernels: 70.8 us -> 63.8 us  [exchange(): pl.pallas_call(exchange_kernel, out_shape=(jax.ShapeDtypeStruct(odd.shape...]
    pallas_call x1, Pallas kernels: 12 us -> 10.5 us  [finish(): pl.pallas_call(finish_kernel, out_shape=(jax.ShapeDtypeStruct((2, TILE_U,...]
where the time goes in v1:
time: 104 us; the launch traced here: 103 us
  Pallas kernels  102 us (98%)
    pallas_call x1, Pallas kernels, exchange(): pl.pallas_call(exchange_kernel, out_shape=(jax.ShapeDtypeStruct(odd.shape...  63.8 us
    pallas_call x1, Pallas kernels, make_outgoing(): pl.pallas_call(screen_kernel, out_shape=(slots, slots, jax.ShapeDtypeStru...  14.2 us
    pallas_call x1, Pallas kernels, borders(): pl.pallas_call(border_kernel, out_shape=(jax.ShapeDtypeStruct(bottom.shap...  11.8 us
    pallas_call x1, Pallas kernels, finish(): pl.pallas_call(finish_kernel, out_shape=(jax.ShapeDtypeStruct((2, TILE_U,...  10.5 us

profile of v1, /device:TPU:0, one launch (start us, length us, event | category | flops | bytes accessed | tf_op | source)
XLA Modules:
  0.0 103.0 jit_solution(6664060701650431537)
XLA Ops:
  0.7 14.2 %screens.1 = (bf16[128,64,128]{2,1,0:T(8,128)(2,1)}, bf16[128,64,128]{2,1,0:T(8,128)(2,1)}, s32[24,128]{1,0:T(8,128)}) custom-call(f32[4]{0:T(128)} %w_hbm.1, s32[2,128]{1,0:T(2,128)} %bitcast.10, bf16[4,512,512]{2,1,0:T(8,128)(2,1)} %amp_hbm.1, bf16[4,512,512]{2,1,0:T(8,128)(2,1)} %phase_hbm.1, f32[2,64,512]{2,1,0:T(8,128)} %constant.2.clone.f_hbm, ...), custom_call_target="tpu_custom_call" | custom-call | flops 2700000000 | bytes 8600000 | tf_op jit(solution)/shard_map/screens/pallas_call | solution.py:148
  14.9 63.8 %exchange.1 = (bf16[128,64,128]{2,1,0:T(8,128)(2,1)}, f32[33,4,256,128]{3,2,1,0:T(8,128)}) custom-call(s32[3072]{0:T(1024)} %bitcast.6, bf16[128,64,128]{2,1,0:T(8,128)(2,1)} %get-tuple-element.17.even_hbm, bf16[128,64,128]{2,1,0:T(8,128)(2,1)} %get-tuple-element.18.odd_hbm, bf16[384,128,128]{2,1,0:T(8,128)(2,1)} %left_hbm.3, bf16[384,64,128]{2,1,0:T(8,128)(2,1)} %right_hbm.3), custom_call_target="tpu_custom_call" | custom-call | tf_op jit(solution)/shard_map/exchange/pallas_call | solution.py:344
  78.7 10.5 %finish.1 = (f32[2,256,512]{2,1,0:T(8,128)}, bf16[2,64,512]{2,1,0:T(8,128)(2,1)}, bf16[320,128]{1,0:T(8,128)(2,1)}) custom-call(s32[3072]{0:T(1024)} %bitcast.7, bf16[128,64,128]{2,1,0:T(8,128)(2,1)} %get-tuple-element.19.recv_hbm, bf16[384,128,128]{2,1,0:T(8,128)(2,1)} %left_hbm.3, bf16[384,64,128]{2,1,0:T(8,128)(2,1)} %right_hbm.3, ...), custom_call_target="tpu_custom_call" | custom-call | flops 1000000000 | bytes 12000000 | tf_op jit(solution)/shard_map/finish/pallas_call | solution.py:472
  89.2 11.8 %borders.1 = (bf16[2,64,512]{2,1,0:T(8,128)(2,1)}, bf16[256,128]{1,0:T(8,128)(2,1)}, bf16[64,128]{1,0:T(8,128)(2,1)}) custom-call(bf16[2,64,512]{2,1,0:T(8,128)(2,1)} %get-tuple-element.22.bottom, bf16[320,128]{1,0:T(8,128)(2,1)} %get-tuple-element.23.side), custom_call_target="tpu_custom_call" | custom-call | tf_op jit(solution)/shard_map/borders/pallas_call | solution.py:519
  101.0 2.0 %join_borders.1 = f32[2,256,512]{2,1,0:T(8,128)} custom-call(f32[2,256,512]{2,1,0:T(8,128)} %get-tuple-element.21.main, bf16[2,64,512]{2,1,0:T(8,128)(2,1)} %get-tuple-element.24.bottom_hbm, bf16[256,128]{1,0:T(8,128)(2,1)} %get-tuple-element.25.side_hbm, bf16[64,128]{1,0:T(8,128)(2,1)} %get-tuple-element.26.corner_hbm), custom_call_target="tpu_custom_call", output_to_operand_aliasing={{}: (0, {})} | custom-call | tf_op jit(solution)/shard_map/join_borders/pallas_call | solution.py:569
